TPU v7x, 256 devices: a whole 4x4x8 slice. The times are simulated.
256 devices in a mesh: rows: 64 (over z, y, core), rep: 4 (over x).
Axes of the slice: x: 4, y: 4, z: 8, core: 2. Of those that a mesh axis runs over, the one named last changes fastest.
Arguments:
- features: bfloat16 [262144, 256], P(('rows', 'rep')), may hold values from -6 to 6
- weight: bfloat16 [256, 256], replicated, may hold values from -0.375 to 0.375
- block_cols: int32 [2048, 4, 2], P('rows', 'rep'), may hold values from 0 to 511, as said below
- block_vals: bfloat16 [2048, 4, 2, 128, 128], P('rows', 'rep'), as said below
- out_grad: bfloat16 [262144, 256], P('rows'), may hold values from -6 to 6
Outputs:
- activations: bfloat16 [262144, 256], P(('rows', 'rep'))
- input_grad: bfloat16 [262144, 256], P(('rows', 'rep'))
- weight_grad: float32 [256, 256], replicated
Inputs may be any that keep to these rules, and one draw needn't show every extreme that they name: `block_cols`: layer c's k-th block column is global block column (k // 8) * 32 + c * 8 + k % 8, whose rows the device of index k // 8 along rows holds in layer c. In the layer that owns a block row, slot 0 is its diagonal block; no other held block of a device lies in its own block columns. For every layer, every device along rows and every other device along rows, at most 1 of the first device's held blocks in that layer lie in block columns of the other, and in every draw some pair has exactly 1. `block_vals`: the adjacency is symmetric: every held block at block row b, block column g in slot s has a partner held at block row g, block column b in slot s (of the layer owning b) that is its transpose; diagonal blocks are symmetric.
All inputs are finite; a program needn't handle non-finite values.
Results may differ from a plain program's by a relative error of at most 0.006.
Values may be sent and summed in bfloat16 or wider, within the bound.
A program may use at most 128 MiB of HBM per device.

v0:
```python
import math
import jax
import jax.numpy as jnp
from jax import lax
from jax.sharding import PartitionSpec as P


def silu_parts(summed):
    sigmoid_vals = jax.nn.sigmoid(summed)
    return (summed * sigmoid_vals, sigmoid_vals * (1.0 + summed * (1.0 - sigmoid_vals)))


def apply_blocks(local_vals, fetched):
    product = jnp.einsum("bsij,bsjf->bif", local_vals, fetched, preferred_element_type=jnp.float32)
    return product.reshape(-1, fetched.shape[-1])


def serve_blocks(source_rows, asked_places, block_size):
    feature_width = source_rows.shape[1]
    blocks = source_rows.reshape(-1, block_size, feature_width)
    flat_ask = asked_places.reshape(-1)
    picked = jnp.take(blocks, jnp.clip(flat_ask, 0, blocks.shape[0] - 1), axis=0)
    picked = jnp.where((flat_ask >= 0)[:, None, None], picked, jnp.zeros_like(picked))
    return picked


def on_device(features, weight, block_cols, block_vals, out_grad):
    own_rows, feature_width = features.shape
    block_size = block_vals.shape[-1]
    row_blocks, slot_count = (block_cols.shape[0], block_cols.shape[2])
    own_blocks = own_rows // block_size
    peer_count = lax.axis_size("rows")
    layer_count = lax.axis_size("rep")
    couple_total = ((layer_count - 1) * slot_count * own_blocks + own_blocks) // 2
    reach_classes = peer_count // 2 - 1
    capacity = (couple_total + reach_classes - 1) // reach_classes
    my_group = lax.axis_index("rows")
    layer_index = lax.axis_index("rep")
    local_vals = block_vals[:, 0]
    flat_cols = block_cols[:, 0].reshape(-1)
    request_total = flat_cols.shape[0]
    owners = flat_cols // own_blocks
    places = flat_cols % own_blocks
    remote = owners != my_group
    positions = jnp.arange(request_total, dtype=jnp.int32)
    same_owner = (owners[:, None] == owners[None, :]) & (positions[:, None] > positions[None, :])
    owner_ranks = jnp.sum(same_owner.astype(jnp.int32), axis=1)
    slot_keys = jnp.where(remote, owners * capacity + owner_ranks, -1)
    slot_table = jnp.arange(peer_count * capacity, dtype=jnp.int32)
    matches = slot_keys[:, None] == slot_table[None, :]
    requests = (jnp.sum(jnp.where(matches, places[:, None] + 1, 0), axis=0) - 1).reshape(
        peer_count, capacity
    )
    asked_places = lax.all_to_all(requests, "rows", split_axis=0, concat_axis=0, tiled=True)
    mixed_rows = jnp.dot(features, weight, preferred_element_type=jnp.float32).astype(jnp.bfloat16)
    arrived = lax.all_to_all(
        serve_blocks(mixed_rows, asked_places, block_size),
        "rows",
        split_axis=0,
        concat_axis=0,
        tiled=True,
    )
    from_peers = jnp.take(arrived, jnp.clip(slot_keys, 0, arrived.shape[0] - 1), axis=0)
    from_self = jnp.take(mixed_rows.reshape(own_blocks, block_size, feature_width), places, axis=0)
    joined = jnp.where(remote[:, None, None], from_peers, from_self)
    partial_sum = apply_blocks(
        local_vals, joined.reshape(row_blocks, slot_count, block_size, feature_width)
    )
    share_start = layer_index * own_rows
    summed = lax.psum(partial_sum, "rep")
    values_all, slopes_all = silu_parts(summed)
    grad_rows = (out_grad.astype(jnp.float32) * slopes_all).astype(jnp.bfloat16)
    activated = lax.dynamic_slice_in_dim(values_all, share_start, own_rows, 0).astype(jnp.bfloat16)
    slot_terms = jnp.einsum(
        "bsji,bjf->bsif",
        local_vals,
        grad_rows.reshape(row_blocks, block_size, feature_width),
        preferred_element_type=jnp.float32,
    ).reshape(request_total, block_size, feature_width)
    filler = jnp.sum(jnp.where(matches, positions[:, None], 0), axis=0)
    filled = jnp.any(matches, axis=0)
    outgoing = jnp.where(
        filled[:, None, None], jnp.take(slot_terms, filler, axis=0), jnp.zeros((), jnp.float32)
    )
    returned = lax.all_to_all(outgoing, "rows", split_axis=0, concat_axis=0, tiled=True)
    block_span = block_size * feature_width
    own_index = jnp.arange(own_blocks, dtype=jnp.int32)
    arrive_hot = (asked_places.reshape(-1)[:, None] == own_index[None, :]).astype(jnp.float32)
    self_hot = ((~remote)[:, None] & (places[:, None] == own_index[None, :])).astype(jnp.float32)
    collected = jnp.einsum(
        "qo,qx->ox", arrive_hot, returned.reshape(-1, block_span), precision=lax.Precision.HIGHEST
    )
    self_terms = jnp.einsum(
        "no,nx->ox", self_hot, slot_terms.reshape(-1, block_span), precision=lax.Precision.HIGHEST
    )
    back_rows = (collected + self_terms).reshape(own_rows, feature_width)
    node_total = own_rows * peer_count * layer_count
    local_weight = jnp.dot(
        features.astype(jnp.float32).T, back_rows, precision=lax.Precision.HIGHEST
    )
    weight_grad = lax.psum(local_weight, ("rows", "rep")) * (1.0 / math.sqrt(node_total))
    input_grad = jnp.dot(
        back_rows.astype(jnp.bfloat16), weight.T, preferred_element_type=jnp.float32
    ).astype(jnp.bfloat16)
    return (activated, input_grad, weight_grad)


def solution(mesh):
    placed = (
        P(("rows", "rep"), None),
        P(),
        P("rows", "rep", None),
        P("rows", "rep", None, None, None),
        P("rows", None),
    )
    return jax.shard_map(
        on_device,
        mesh=mesh,
        in_specs=placed,
        out_specs=(P(("rows", "rep"), None), P(("rows", "rep"), None), P()),
        check_vma=False,
    )
```

profile of v0, /device:TPU:2, one launch (start us, length us, event | category | flops | bytes accessed | tf_op | source)
XLA Modules:
  0.0 755.1 jit_solution(3216159301547902736)
XLA Ops:
  7.2 0.9 copy.37
  9.3 12.1 %all-to-all-start = ((s32[64,1,1]{2,1,0:T(1,128)}), s32[64,1,1]{2,1,0:T(1,128)S(1)}, u32[]{:S(2)}, u32[]{:S(2)}) async-start(s32[64,1,1]{2,1,0:T(1,128)} %copy.38), calls=%async_computation | async-start | bytes 65536 | tf_op jit(solution)/shard_map/all_to_all | solution.py:54
  21.4 1.4 convolution_convert_fusion.1
  22.7 8.2 %all-to-all-done = s32[64,1,1]{2,1,0:T(1,128)S(1)} async-done(((s32[64,1,1]{2,1,0:T(1,128)}), s32[64,1,1]{2,1,0:T(1,128)S(1)}, u32[]{:S(2)}, u32[]{:S(2)}) %all-to-all-start) | async-done | bytes 288 | tf_op jit(solution)/shard_map/all_to_all | solution.py:54
  30.9 1.2 reduce.1
  32.1 2.8 gather_fusion.2
  34.9 1.2 compare_reduce_fusion
  36.1 4.0 select_select_fusion.2
  40.1 5.7 all-to-all-start.1
  46.1 2.8 gather_fusion.3
  48.9 93.1 %all-to-all-done.1 = bf16[64,128,256]{2,1,0:T(8,128)(2,1)} async-done(((bf16[64,128,256]{2,1,0:T(8,128)(2,1)}), bf16[64,128,256]{2,1,0:T(8,128)(2,1)}, u32[]{:S(2)}, u32[]{:S(2)}) %all-to-all-start.1) | async-done | bytes 4194336 | tf_op jit(solution)/shard_map/all_to_all | solution.py:56
  142.0 5.0 gather_fusion
  147.0 4.1 select_select_fusion.1
  151.0 2.8 fusion.2
  154.0 92.9 %all-reduce.3.cloned.1.call-done = f32[4096,256]{1,0:T(8,128)} async-done(((f32[4096,256]{1,0:T(8,128)}), f32[4096,256]{1,0:T(8,128)}) %all-reduce.3.cloned.1.call-update) | async-done | bytes 4194320 | tf_op jit(solution)/shard_map/psum | solution.py:70
  246.9 6.4 multiply_convert_fusion
  253.3 4.5 fusion
  257.9 9.0 %copy.41 = f32[64,128,256]{2,1,0:T(8,128)} copy(f32[64,128,256]{1,2,0:T(8,128)} %bitcast.59) | data formatting | bytes 16777216 | tf_op jit(solution)/shard_map/reshape | solution.py:79
  266.9 7.7 %gather_fusion.1 = f32[64,128,256]{2,1,0:T(8,128)} fusion(f32[64,128,256]{2,1,0:T(8,128)} %copy.41, s32[1024]{0:T(1024)S(1)} %pad_clamp_fusion), kind=kCustom, calls=%fused_computation.3 | custom fusion | bytes 16777472 | tf_op jit(solution)/shard_map/jit(_take)/gather | solution.py:83
  274.5 8.5 %select_select_fusion = f32[64,128,256]{2,1,0:T(8,128)} fusion(f32[64,128,256]{2,1,0:T(8,128)} %gather_fusion.1, pred[64]{0:T(512)(128)(4,1)S(1)} %compare_and_fusion.2, pred[64]{0:T(512)(128)(4,1)S(1)} %fusion.6), kind=kLoop, calls=%fused_computation.5 | loop fusion | flops 4194304 | bytes 16777344 | tf_op jit(solution)/shard_map/jit(_where)/select_n | solution.py:82
  283.0 10.7 %all-to-all-start.2 = ((f32[64,128,256]{2,1,0:T(8,128)}), f32[64,128,256]{2,1,0:T(8,128)}, u32[]{:S(2)}, u32[]{:S(2)}) async-start(f32[64,128,256]{2,1,0:T(8,128)} %select_select_fusion), calls=%async_computation.2 | async-start | bytes 16777216 | tf_op jit(solution)/shard_map/all_to_all | solution.py:85
  293.8 9.2 %copy.49 = f32[8,8,128,256]{3,1,2,0:T(8,128)} copy(f32[8,8,128,256]{2,3,1,0:T(8,128)} %bitcast.60) | data formatting | bytes 16777216
  303.0 2.4 fusion.4
  305.5 174.4 %all-to-all-done.2 = f32[64,128,256]{2,1,0:T(8,128)} async-done(((f32[64,128,256]{2,1,0:T(8,128)}), f32[64,128,256]{2,1,0:T(8,128)}, u32[]{:S(2)}, u32[]{:S(2)}) %all-to-all-start.2) | async-done | bytes 8388640 | tf_op jit(solution)/shard_map/all_to_all | solution.py:85
  479.9 8.3 %copy.48 = f32[8,8,128,256]{3,1,2,0:T(8,128)S(1)} copy(f32[8,8,128,256]{3,2,1,0:T(8,128)} %bitcast.25) | data formatting | bytes 16777216
  488.1 2.9 fusion.8
  491.1 3.9 convolution_add_fusion
  494.9 1.4 reshape.298
  496.4 2.7 convolution_bitcast_fusion
  499.1 1.1 convolution_convert_fusion
  500.3 246.2 %all-reduce.5.cloned.1.call-done = f32[256,256]{0,1:T(8,128)} async-done(((f32[256,256]{0,1:T(8,128)}), f32[256,256]{0,1:T(8,128)}) %all-reduce.5.cloned.1.call-update) | async-done | bytes 262160 | tf_op jit(solution)/shard_map/psum | solution.py:101
  746.4 1.0 broadcast_multiply_fusion
  (34 shorter events, 2.6 us)
Async XLA Ops:
  7.2 143.9 %copy-start = (bf16[32,1,2,128,128]{4,3,2,1,0:T(8,128)(2,1)S(1)}, bf16[32,1,2,128,128]{4,3,2,1,0:T(8,128)(2,1)}, u32[]{:S(2)}) copy-start(bf16[32,1,2,128,128]{4,3,2,1,0:T(8,128)(2,1)} %param.10) | copy-start | bytes 6291460
  9.3 21.6 %all-to-all-start = ((s32[64,1,1]{2,1,0:T(1,128)}), s32[64,1,1]{2,1,0:T(1,128)S(1)}, u32[]{:S(2)}, u32[]{:S(2)}) async-start(s32[64,1,1]{2,1,0:T(1,128)} %copy.38), calls=%async_computation | async-start | bytes 65536 | tf_op jit(solution)/shard_map/all_to_all | solution.py:54
  40.1 101.9 %all-to-all-start.1 = ((bf16[64,128,256]{2,1,0:T(8,128)(2,1)}), bf16[64,128,256]{2,1,0:T(8,128)(2,1)}, u32[]{:S(2)}, u32[]{:S(2)}) async-start(bf16[64,128,256]{2,1,0:T(8,128)(2,1)} %select_select_fusion.2), calls=%async_computation.1 | async-start | bytes 8388608 | tf_op jit(solution)/shard_map/all_to_all | solution.py:56
  45.8 201.1 %all-reduce.3.cloned.1.call-start = ((), (), s32[]{:S(2)}) async-start(), calls=%async_computation.3 | async-start | bytes 8388608 | tf_op jit(solution)/shard_map/psum | solution.py:70
  283.0 196.8 %all-to-all-start.2 = ((f32[64,128,256]{2,1,0:T(8,128)}), f32[64,128,256]{2,1,0:T(8,128)}, u32[]{:S(2)}, u32[]{:S(2)}) async-start(f32[64,128,256]{2,1,0:T(8,128)} %select_select_fusion), calls=%async_computation.2 | async-start | bytes 16777216 | tf_op jit(solution)/shard_map/all_to_all | solution.py:85
  293.8 452.7 %all-reduce.5.cloned.1.call-start = ((), (), s32[]{:S(2)}) async-start(), calls=%async_computation.4 | async-start | bytes 524288 | tf_op jit(solution)/shard_map/psum | solution.py:101
  479.8 11.2 %slice-start = ((s8[8388608]{0:T(1024)(128)(4,1)}), s8[4194304]{0:T(1024)(128)(4,1)S(1)}, s32[]{:S(2)}) async-start(s8[8388608]{0:T(1024)(128)(4,1)} %bitcast.63), calls=%async_computation.5 | async-start | bytes 8388608
  479.9 11.2 %slice-start.1 = ((s8[8388608]{0:T(1024)(128)(4,1)}), s8[4194304]{0:T(1024)(128)(4,1)S(1)}, s32[]{:S(2)}) async-start(s8[8388608]{0:T(1024)(128)(4,1)} %bitcast.63), calls=%async_computation.6 | async-start | bytes 8388608
  491.0 257.2 %copy-start.1 = (bf16[32,1,2,128,128]{4,3,2,1,0:T(8,128)(2,1)S(1)}, bf16[32,1,2,128,128]{4,3,2,1,0:T(8,128)(2,1)}, u32[]{:S(2)}) copy-start(bf16[32,1,2,128,128]{4,3,2,1,0:T(8,128)(2,1)} %param.10) | copy-start | bytes 6291460
  494.9 4.2 copy-start.2
Sparse Core Ops, SparseCore 0:
  154.0 92.8 all-reduce.2
  499.2 247.1 all-reduce.4
where the time goes:
time: 756 us; the launch traced here: 755 us
  waiting for transfers between devices  615 us (81%)
  local copies, waits for them, and re-layouts  48.7 us (6%)
  other arithmetic  29.3 us (4%)
  starting transfers between devices  28.8 us (4%)
  matrix products  19.3 us (3%)
  between operations  14.2 us (2%)
    psum x1, waiting for transfers between devices, on_device(): lax.psum(local_weight, ('rows', 'rep')) * (1.0 / math.sqrt(node_total))  246 us
    all_to_all x1, waiting for transfers between devices, on_device(): lax.all_to_all(outgoing, 'rows', split_axis=0, concat_axis=0, tiled=True)  174 us
    all_to_all x1, waiting for transfers between devices, on_device(): lax.all_to_all(serve_blocks(mixed_rows, asked_places, block_size), 'rows'...  93.1 us
    psum x1, waiting for transfers between devices, on_device(): summed = lax.psum(partial_sum, 'rep')  92.9 us
    unnamed x14, local copies, waits for them, and re-layouts  19.2 us
  transfers between devices with their start and end apart: 5, of which 5 were waited for; matrix products, arithmetic and copies ran while one was open for 2% of the time, Pallas kernels for 0%

commit v1 on v0

--- a/solution.py
+++ b/solution.py
@@ -98,7 +98,7 @@
     local_weight = jnp.dot(
         features.astype(jnp.float32).T, back_rows, precision=lax.Precision.HIGHEST
     )
-    weight_grad = lax.psum(local_weight, ("rows", "rep")) * (1.0 / math.sqrt(node_total))
+    weight_grad = lax.psum(lax.psum(local_weight, "rows"), "rep") * (1.0 / math.sqrt(node_total))
     input_grad = jnp.dot(
         back_rows.astype(jnp.bfloat16), weight.T, preferred_element_type=jnp.float32
     ).astype(jnp.bfloat16)

time: 756 us -> 727 us (0.962)
  waiting for transfers between devices: 615 us -> 585 us
    psum x1 -> x2, waiting for transfers between devices: 246 us -> 214 us  [the longest x1 168 us: on_device(): lax.psum(local_weight, 'rows')]
  transfers between devices with their start and end apart: 5 -> 6, of which waited for: 5 -> 6; matrix products, arithmetic and copies ran while one was open for 2% -> 2% of each run, Pallas kernels for 0% -> 0%
where the time goes in v1:
time: 727 us; the launch traced here: 725 us
  waiting for transfers between devices  585 us (80%)
  local copies, waits for them, and re-layouts  48.9 us (7%)
  other arithmetic  29.3 us (4%)
  starting transfers between devices  28.8 us (4%)
  matrix products  19.3 us (3%)
  between operations  13.9 us (2%)
    all_to_all x1, waiting for transfers between devices, on_device(): lax.all_to_all(outgoing, 'rows', split_axis=0, concat_axis=0, tiled=True)  177 us
    psum x1, waiting for transfers between devices, on_device(): lax.psum(local_weight, 'rows')  168 us
    all_to_all x1, waiting for transfers between devices, on_device(): lax.all_to_all(serve_blocks(mixed_rows, asked_places, block_size), 'rows'...  93.1 us
    psum x1, waiting for transfers between devices, on_device(): summed = lax.psum(partial_sum, 'rep')  92.9 us
    psum x1, waiting for transfers between devices, on_device(): lax.psum(lax.psum(local_weight, 'rows'), 'rep')  45.5 us
    unnamed x14, local copies, waits for them, and re-layouts  19.2 us
  transfers between devices with their start and end apart: 6, of which 6 were waited for; matrix products, arithmetic and copies ran while one was open for 2% of the time, Pallas kernels for 0%

profile of v1, /device:TPU:2, one launch (start us, length us, event | category | flops | bytes accessed | tf_op | source)
XLA Modules:
  0.0 725.1 jit_solution(11280827492853523220)
XLA Ops:
  9.3 12.1 %all-to-all-start = ((s32[64,1,1]{2,1,0:T(1,128)}), s32[64,1,1]{2,1,0:T(1,128)S(1)}, u32[]{:S(2)}, u32[]{:S(2)}) async-start(s32[64,1,1]{2,1,0:T(1,128)} %copy.38), calls=%async_computation | async-start | bytes 65536 | tf_op jit(solution)/shard_map/all_to_all | solution.py:54
  21.4 1.4 convolution_convert_fusion.1
  22.7 8.2 %all-to-all-done = s32[64,1,1]{2,1,0:T(1,128)S(1)} async-done(((s32[64,1,1]{2,1,0:T(1,128)}), s32[64,1,1]{2,1,0:T(1,128)S(1)}, u32[]{:S(2)}, u32[]{:S(2)}) %all-to-all-start) | async-done | bytes 288 | tf_op jit(solution)/shard_map/all_to_all | solution.py:54
  30.9 1.2 reduce.1
  32.1 2.8 gather_fusion.2
  34.9 1.2 compare_reduce_fusion
  36.1 4.0 select_select_fusion.2
  40.1 5.7 all-to-all-start.1
  46.1 2.8 gather_fusion.3
  48.9 93.1 %all-to-all-done.1 = bf16[64,128,256]{2,1,0:T(8,128)(2,1)} async-done(((bf16[64,128,256]{2,1,0:T(8,128)(2,1)}), bf16[64,128,256]{2,1,0:T(8,128)(2,1)}, u32[]{:S(2)}, u32[]{:S(2)}) %all-to-all-start.1) | async-done | bytes 4194336 | tf_op jit(solution)/shard_map/all_to_all | solution.py:56
  142.0 5.0 gather_fusion
  147.0 4.1 select_select_fusion.1
  151.0 2.8 fusion.2
  154.0 92.9 %all-reduce.4.cloned.1.call-done = f32[4096,256]{1,0:T(8,128)} async-done(((f32[4096,256]{1,0:T(8,128)}), f32[4096,256]{1,0:T(8,128)}) %all-reduce.4.cloned.1.call-update) | async-done | bytes 4194320 | tf_op jit(solution)/shard_map/psum | solution.py:70
  246.9 6.4 multiply_convert_fusion
  253.3 4.5 fusion
  257.9 9.0 %copy.41 = f32[64,128,256]{2,1,0:T(8,128)} copy(f32[64,128,256]{1,2,0:T(8,128)} %bitcast.59) | data formatting | bytes 16777216 | tf_op jit(solution)/shard_map/reshape | solution.py:79
  266.9 7.7 %gather_fusion.1 = f32[64,128,256]{2,1,0:T(8,128)} fusion(f32[64,128,256]{2,1,0:T(8,128)} %copy.41, s32[1024]{0:T(1024)S(1)} %pad_clamp_fusion), kind=kCustom, calls=%fused_computation.3 | custom fusion | bytes 16777472 | tf_op jit(solution)/shard_map/jit(_take)/gather | solution.py:83
  274.5 8.5 %select_select_fusion = f32[64,128,256]{2,1,0:T(8,128)} fusion(f32[64,128,256]{2,1,0:T(8,128)} %gather_fusion.1, pred[64]{0:T(512)(128)(4,1)S(1)} %compare_and_fusion.2, pred[64]{0:T(512)(128)(4,1)S(1)} %fusion.6), kind=kLoop, calls=%fused_computation.5 | loop fusion | flops 4194304 | bytes 16777344 | tf_op jit(solution)/shard_map/jit(_where)/select_n | solution.py:82
  283.0 10.7 %all-to-all-start.2 = ((f32[64,128,256]{2,1,0:T(8,128)}), f32[64,128,256]{2,1,0:T(8,128)}, u32[]{:S(2)}, u32[]{:S(2)}) async-start(f32[64,128,256]{2,1,0:T(8,128)} %select_select_fusion), calls=%async_computation.2 | async-start | bytes 16777216 | tf_op jit(solution)/shard_map/all_to_all | solution.py:85
  293.8 9.2 %copy.49 = f32[8,8,128,256]{3,1,2,0:T(8,128)} copy(f32[8,8,128,256]{2,3,1,0:T(8,128)} %bitcast.60) | data formatting | bytes 16777216
  303.0 176.8 %all-to-all-done.2 = f32[64,128,256]{2,1,0:T(8,128)} async-done(((f32[64,128,256]{2,1,0:T(8,128)}), f32[64,128,256]{2,1,0:T(8,128)}, u32[]{:S(2)}, u32[]{:S(2)}) %all-to-all-start.2) | async-done | bytes 8388640 | tf_op jit(solution)/shard_map/all_to_all | solution.py:85
  479.9 8.3 %copy.48 = f32[8,8,128,256]{3,1,2,0:T(8,128)S(1)} copy(f32[8,8,128,256]{3,2,1,0:T(8,128)} %bitcast.25) | data formatting | bytes 16777216
  488.1 2.9 fusion.8
  491.0 3.9 convolution_add_fusion
  494.9 1.5 reshape.298
  496.5 2.7 convolution_bitcast_fusion
  499.3 2.4 fusion.4
  501.7 168.4 %all-reduce.6.cloned.1.call-done = f32[256,256]{0,1:T(8,128)} async-done(((f32[256,256]{0,1:T(8,128)}), f32[256,256]{0,1:T(8,128)}) %all-reduce.6.cloned.1.call-update) | async-done | bytes 262160 | tf_op jit(solution)/shard_map/psum | solution.py:101
  670.1 1.1 convolution_convert_fusion
  671.3 45.5 %all-reduce.8.cloned.1.call-done = f32[256,256]{0,1:T(8,128)} async-done(((f32[256,256]{0,1:T(8,128)}), f32[256,256]{0,1:T(8,128)}) %all-reduce.8.cloned.1.call-update) | async-done | bytes 262160 | tf_op jit(solution)/shard_map/psum | solution.py:101
  716.8 1.0 broadcast_multiply_fusion
  (37 shorter events, 3.5 us)
Async XLA Ops:
  7.2 143.9 %copy-start = (bf16[32,1,2,128,128]{4,3,2,1,0:T(8,128)(2,1)S(1)}, bf16[32,1,2,128,128]{4,3,2,1,0:T(8,128)(2,1)}, u32[]{:S(2)}) copy-start(bf16[32,1,2,128,128]{4,3,2,1,0:T(8,128)(2,1)} %param.10) | copy-start | bytes 6291460
  9.3 21.6 %all-to-all-start = ((s32[64,1,1]{2,1,0:T(1,128)}), s32[64,1,1]{2,1,0:T(1,128)S(1)}, u32[]{:S(2)}, u32[]{:S(2)}) async-start(s32[64,1,1]{2,1,0:T(1,128)} %copy.38), calls=%async_computation | async-start | bytes 65536 | tf_op jit(solution)/shard_map/all_to_all | solution.py:54
  40.1 101.9 %all-to-all-start.1 = ((bf16[64,128,256]{2,1,0:T(8,128)(2,1)}), bf16[64,128,256]{2,1,0:T(8,128)(2,1)}, u32[]{:S(2)}, u32[]{:S(2)}) async-start(bf16[64,128,256]{2,1,0:T(8,128)(2,1)} %select_select_fusion.2), calls=%async_computation.1 | async-start | bytes 8388608 | tf_op jit(solution)/shard_map/all_to_all | solution.py:56
  45.8 201.1 %all-reduce.4.cloned.1.call-start = ((), (), s32[]{:S(2)}) async-start(), calls=%async_computation.3 | async-start | bytes 8388608 | tf_op jit(solution)/shard_map/psum | solution.py:70
  283.0 196.8 %all-to-all-start.2 = ((f32[64,128,256]{2,1,0:T(8,128)}), f32[64,128,256]{2,1,0:T(8,128)}, u32[]{:S(2)}, u32[]{:S(2)}) async-start(f32[64,128,256]{2,1,0:T(8,128)} %select_select_fusion), calls=%async_computation.2 | async-start | bytes 16777216 | tf_op jit(solution)/shard_map/all_to_all | solution.py:85
  293.8 376.3 %all-reduce.6.cloned.1.call-start = ((), (), s32[]{:S(2)}) async-start(), calls=%async_computation.4 | async-start | bytes 524288 | tf_op jit(solution)/shard_map/psum | solution.py:101
  479.8 11.2 %slice-start = ((s8[8388608]{0:T(1024)(128)(4,1)}), s8[4194304]{0:T(1024)(128)(4,1)S(1)}, s32[]{:S(2)}) async-start(s8[8388608]{0:T(1024)(128)(4,1)} %bitcast.63), calls=%async_computation.6 | async-start | bytes 8388608
  479.9 11.2 %slice-start.1 = ((s8[8388608]{0:T(1024)(128)(4,1)}), s8[4194304]{0:T(1024)(128)(4,1)S(1)}, s32[]{:S(2)}) async-start(s8[8388608]{0:T(1024)(128)(4,1)} %bitcast.63), calls=%async_computation.7 | async-start | bytes 8388608
  494.9 175.2 %copy-start.2 = (bf16[256,256]{1,0:T(8,128)(2,1)S(1)}, bf16[256,256]{1,0:T(8,128)(2,1)}, u32[]{:S(2)}) copy-start(bf16[256,256]{1,0:T(8,128)(2,1)} %param.8) | copy-start | bytes 393220
  494.9 223.7 %copy-start.1 = (bf16[32,1,2,128,128]{4,3,2,1,0:T(8,128)(2,1)S(1)}, bf16[32,1,2,128,128]{4,3,2,1,0:T(8,128)(2,1)}, u32[]{:S(2)}) copy-start(bf16[32,1,2,128,128]{4,3,2,1,0:T(8,128)(2,1)} %param.10) | copy-start | bytes 6291460
  499.2 217.6 %all-reduce.8.cloned.1.call-start = ((), (), s32[]{:S(2)}) async-start(), calls=%async_computation.5 | async-start | bytes 524288 | tf_op jit(solution)/shard_map/psum | solution.py:101
Sparse Core Ops, SparseCore 0:
  154.0 92.8 all-reduce.3
  499.4 170.6 all-reduce.5
  672.4 44.3 all-reduce.7
